TPU v7x, 128 devices: a whole 4x4x4 slice. The times are simulated.
128 devices in a mesh: section: 4 (over z_lo, core), expert: 32 (over y, x, z_hi).
Axes of the slice: x: 4, y: 4, z: 4 (z_hi: 2, z_lo: 2; z = z_hi * 2 + z_lo), core: 2. Of those that a mesh axis runs over, the one named last changes fastest.
Arguments:
- tokens: bfloat16 [4, 2048, 4096], P('section', 'expert'), may hold values from -6 to 6
- out_grad: bfloat16 [4, 2048, 4096], P('section', 'expert'), may hold values from -6 to 6
- expert_ids: int32 [4, 2048, 2], P('section', 'expert'), may hold values from 0 to 7, as said below
- slot_ids: int32 [4, 2048, 2], P('section', 'expert'), may hold values from 0 to 15, as said below
- gate_int: int32 [4, 2048, 2], P('section', 'expert'), may hold values from 16 to 255
- saved_gate: bfloat16 [4, 512, 14336], P('section', None, 'expert'), may hold values from -6 to 6
- saved_up: bfloat16 [4, 512, 14336], P('section', None, 'expert'), may hold values from -6 to 6
- w_gate: bfloat16 [4, 4096, 14336], P('section', None, 'expert'), may hold values from -0.09375 to 0.09375
- w_up: bfloat16 [4, 4096, 14336], P('section', None, 'expert'), may hold values from -0.09375 to 0.09375
- w_down: bfloat16 [4, 14336, 4096], P('section', 'expert'), may hold values from -0.0625 to 0.0625
Outputs:
- arriving_grad: bfloat16 [4, 2048, 4096], P('section', 'expert')
- grad_w_gate: bfloat16 [4, 4096, 14336], P('section', None, 'expert')
- grad_w_up: bfloat16 [4, 4096, 14336], P('section', None, 'expert')
- grad_w_down: bfloat16 [4, 14336, 4096], P('section', 'expert')
Inputs may be any that keep to these rules, and one draw needn't show every extreme that they name: `expert_ids`: in each section, the 64 tokens of each index of expert name each of the 8 experts exactly 16 times; a token's two experts differ. `slot_ids`: for each expert, the slots of the 64 tokens of one index of expert that name it are 0 to 15, each once.
All inputs are finite; a program needn't handle non-finite values.
Results may differ from a plain program's by a relative error of at most 0.018.
Values may be sent and summed in bfloat16 or wider, within the bound.
A program may use at most 128 MiB of HBM per device.

v0:
```python
import jax
import jax.numpy as jnp
from jax import lax
from jax.sharding import PartitionSpec as P

EXPERTS = 8
E_WIN = 2


def from_behind(x, axis, by):
    peers = lax.axis_size(axis)
    pairs = [(i, i + by) for i in range(peers) if 0 <= i + by < peers]
    return lax.ppermute(x, axis, pairs)


def shards(
    tokens, out_grad, expert_ids, slot_ids, gate_int, saved_gate, saved_up, w_gate, w_up, w_down
):
    inputs = tokens[0]
    upstream_grad = out_grad[0]
    chosen = expert_ids[0]
    places = slot_ids[0]
    weights_k = gate_int[0].astype(jnp.float32) / 256.0
    devices = lax.axis_size("expert")
    per_expert = devices // E_WIN
    capacity = inputs.shape[0] * 2 // EXPERTS
    slot_count = E_WIN * capacity
    model_width = inputs.shape[1]
    target = chosen * capacity + places
    columns = lax.broadcasted_iota(jnp.int32, (1, 1, slot_count), 2)
    placed = jnp.logical_and(target[:, :, None] == columns, chosen[:, :, None] < E_WIN).astype(
        jnp.float32
    )
    selector = jnp.sum(placed, axis=1)
    scaled = jnp.sum(placed * weights_k[:, :, None], axis=1)
    send_inputs = jnp.einsum(
        "tc,td->cd", selector.astype(jnp.bfloat16), inputs, preferred_element_type=jnp.float32
    ).astype(jnp.bfloat16)
    send_grads = jnp.einsum(
        "tc,td->cd", scaled.astype(jnp.bfloat16), upstream_grad, preferred_element_type=jnp.float32
    ).astype(jnp.bfloat16)
    send_inputs = jnp.repeat(send_inputs.reshape(E_WIN, capacity, model_width), per_expert, axis=0)
    send_grads = jnp.repeat(send_grads.reshape(E_WIN, capacity, model_width), per_expert, axis=0)
    recv_inputs, recv_grads = (
        lax.all_to_all(send_inputs, "expert", split_axis=0, concat_axis=0, tiled=True),
        lax.all_to_all(send_grads, "expert", split_axis=0, concat_axis=0, tiled=True),
    )
    rows_in = recv_inputs.reshape(-1, model_width)
    rows_grad = recv_grads.reshape(-1, model_width)
    gate_pre = saved_gate[0].astype(jnp.float32)
    up_pre = saved_up[0].astype(jnp.float32)
    sigmoid_g = jax.nn.sigmoid(gate_pre)
    activated = gate_pre * sigmoid_g
    hidden = (activated * up_pre).astype(jnp.bfloat16)
    hidden_grad = jnp.einsum("rd,hd->rh", rows_grad, w_down[0], preferred_element_type=jnp.float32)
    gate_grad = (hidden_grad * up_pre * sigmoid_g * (1.0 + gate_pre * (1.0 - sigmoid_g))).astype(
        jnp.bfloat16
    )
    up_grad = (hidden_grad * activated).astype(jnp.bfloat16)
    partial_rows = jnp.einsum("rh,dh->rd", gate_grad, w_gate[0], preferred_element_type=jnp.float32)
    partial_rows = (
        partial_rows + jnp.einsum("rh,dh->rd", up_grad, w_up[0], preferred_element_type=jnp.float32)
    ).astype(jnp.bfloat16)
    grad_down = jnp.einsum(
        "rh,rd->hd", hidden, rows_grad, preferred_element_type=jnp.float32
    ).astype(jnp.bfloat16)
    grad_gate = jnp.einsum(
        "rd,rh->dh", rows_in, gate_grad, preferred_element_type=jnp.float32
    ).astype(jnp.bfloat16)
    grad_up = jnp.einsum("rd,rh->dh", rows_in, up_grad, preferred_element_type=jnp.float32).astype(
        jnp.bfloat16
    )
    own_expert = lax.axis_index("expert") // per_expert
    expert_mask = (lax.iota(jnp.int32, E_WIN) == own_expert).astype(jnp.float32)
    padded = (
        partial_rows.astype(jnp.float32).reshape(devices, 1, capacity, model_width)
        * expert_mask[None, :, None, None]
    )
    summed = lax.psum_scatter(
        padded.astype(jnp.bfloat16), "expert", scatter_dimension=0, tiled=True
    ).astype(jnp.float32)[0]
    combined = jnp.einsum(
        "tc,cd->td",
        selector,
        summed.reshape(slot_count, model_width),
        precision=lax.Precision.HIGHEST,
    ).astype(jnp.bfloat16)
    arriving = from_behind(combined, "section", -1)
    return (arriving[None], grad_gate[None], grad_up[None], grad_down[None])


def solution(mesh):
    return jax.shard_map(
        shards,
        mesh=mesh,
        in_specs=(
            P("section", "expert", None),
            P("section", "expert", None),
            P("section", "expert", None),
            P("section", "expert", None),
            P("section", "expert", None),
            P("section", None, "expert"),
            P("section", None, "expert"),
            P("section", None, "expert"),
            P("section", None, "expert"),
            P("section", "expert", None),
        ),
        out_specs=(
            P("section", "expert", None),
            P("section", None, "expert"),
            P("section", None, "expert"),
            P("section", "expert", None),
        ),
        check_vma=False,
    )
```

profile of v0, /device:TPU:1, one launch (start us, length us, event | category | flops | bytes accessed | tf_op | source)
XLA Modules:
  0.0 372.6 jit_solution(7467593786854591955)
XLA Ops:
  7.2 0.7 multiply_bitcast_fusion
  7.9 0.7 compare_bitcast_fusion
  8.6 0.7 add_bitcast_fusion
  9.3 0.2 convolution_convert_fusion.5
  9.6 2.5 broadcast_in_dim.21
  12.0 11.4 %all-to-all-start = ((bf16[32,16,4096]{2,1,0:T(8,128)(2,1)}), bf16[32,16,4096]{2,1,0:T(8,128)(2,1)}, u32[]{:S(2)}, u32[]{:S(2)}) async-start(bf16[32,16,4096]{2,1,0:T(8,128)(2,1)} %bitcast.89), calls=%async_computation | async-start | bytes 8388608 | tf_op jit(solution)/shard_map/all_to_all | solution.py:46
  23.5 0.0 reduce-scatter.2.cloned.1.call-start
  23.5 60.1 %all-to-all-done = bf16[32,16,4096]{2,1,0:T(8,128)(2,1)} async-done(((bf16[32,16,4096]{2,1,0:T(8,128)(2,1)}), bf16[32,16,4096]{2,1,0:T(8,128)(2,1)}, u32[]{:S(2)}, u32[]{:S(2)}) %all-to-all-start) | async-done | bytes 4194336 | tf_op jit(solution)/shard_map/all_to_all | solution.py:46
  83.7 5.7 %fusion.14 = (bf16[512,448]{0,1:T(8,128)(2,1)S(1)}, f32[512,448]{0,1:T(8,128)S(1)}) fusion(bf16[1,512,448]{1,2,0:T(8,128)(2,1)S(1)} %copy-done.5, bf16[1,512,448]{1,2,0:T(8,128)(2,1)S(1)} %copy-done.6, bf16[512,4096]{1,0:T(8,128)(2,1)} %bitcast.6, bf16[1,448,4096]{2,1,0:T(8,128)(2,1)} %param.19), kind=kOutput, calls=%fused_computation.27 | convolution fusion | flops 1881800704 | bytes 10158080 | tf_op jit(solution)/shard_map/rd,hd->rh/dot_general | solution.py:55
  89.4 2.4 fusion.4
  91.8 2.7 add_convert_fusion
  94.6 4.3 %convert.3 = f32[32,16,4096]{2,1,0:T(8,128)} convert(bf16[32,16,4096]{2,1,0:T(8,128)(2,1)S(1)} %bitcast.91) | non-fusion elementwise | flops 2097152 | bytes 12582912 | tf_op jit(solution)/shard_map/mul | solution.py:76
  98.9 8.4 %multiply_convert_fusion = bf16[32,2,16,4096]{3,2,1,0:T(8,128)(2,1)} fusion(f32[2]{0:T(128)S(1)} %compare_convert_fusion, f32[32,16,4096]{2,1,0:T(8,128)} %convert.3), kind=kLoop, calls=%fused_computation | loop fusion | flops 8388608 | bytes 16777224 | tf_op jit(solution)/shard_map/convert_element_type | solution.py:80
  107.3 1.0 copy-done.3
  108.3 0.2 convolution_convert_fusion.4
  108.6 0.5 broadcast_in_dim.23
  109.1 62.9 %all_to_all.10 = bf16[32,16,4096]{2,1,0:T(8,128)(2,1)S(1)} all-to-all(bf16[32,16,4096]{2,1,0:T(8,128)(2,1)S(1)} %bitcast.90), channel_id=1, replica_groups=mesh['section'=4,'expert'=32] {'expert'}, dimensions={0} | all-to-all | bytes 8388608 | tf_op jit(solution)/shard_map/all_to_all | solution.py:45
  172.0 3.9 %fusion.1 = bf16[1,4096,448]{1,2,0:T(8,128)(2,1)} fusion(bf16[512,448]{0,1:T(8,128)(2,1)S(1)} %get-tuple-element.6, bf16[512,4096]{1,0:T(8,128)(2,1)S(1)} %bitcast.92), kind=kOutput, calls=%fused_computation.6 | convolution fusion | flops 1880883200 | bytes 8323072 | tf_op jit(solution)/shard_map/rd,rh->dh/dot_general | solution.py:67
  175.9 4.0 %fusion.2 = bf16[1,4096,448]{1,2,0:T(8,128)(2,1)} fusion(bf16[512,4096]{1,0:T(8,128)(2,1)S(1)} %bitcast.93, f32[512,448]{0,1:T(8,128)S(1)} %get-tuple-element.7, bf16[1,512,448]{1,2,0:T(8,128)(2,1)S(1)} %copy-done.6), kind=kOutput, calls=%fused_computation.7 | convolution fusion | flops 1882488832 | bytes 9240576 | tf_op jit(solution)/shard_map/rd,rh->dh/dot_general | solution.py:70
  179.8 154.1 %reduce-scatter.2.cloned.1.call-done = bf16[1,2,16,4096]{3,2,1,0:T(8,128)(2,1)} async-done(((bf16[32,2,16,4096]{3,2,1,0:T(8,128)(2,1)}), bf16[1,2,16,4096]{3,2,1,0:T(8,128)(2,1)}) %reduce-scatter.2.cloned.1.call-update) | async-done | bytes 262160 | tf_op jit(solution)/shard_map/reduce_scatter | solution.py:79
  334.0 1.6 convolution_convert_fusion.3
  335.6 23.2 %collective-permute-start = (bf16[64,4096]{1,0:T(8,128)(2,1)S(1)}, bf16[64,4096]{1,0:T(8,128)(2,1)S(1)}, u32[]{:S(2)}, u32[]{:S(2)}) collective-permute-start(bf16[64,4096]{1,0:T(8,128)(2,1)S(1)} %convolution_convert_fusion.3), channel_id=1, source_target_pairs={{32,0},{64,32},{96,64},{33,1},{65,33},{97,65},{34,2},{66,34},{98,6... | collective-permute-start | bytes 1572872 | tf_op jit(solution)/shard_map/ppermute | solution.py:13
  358.8 6.2 %fusion = bf16[1,448,4096]{2,1,0:T(8,128)(2,1)} fusion(bf16[512,4096]{1,0:T(8,128)(2,1)} %bitcast.6, bf16[1,512,448]{1,2,0:T(8,128)(2,1)S(1)} %copy-done.5, bf16[1,512,448]{1,2,0:T(8,128)(2,1)S(1)} %copy-done.6), kind=kOutput, calls=%fused_computation.5 | convolution fusion | flops 1882718208 | bytes 8781824 | tf_op jit(solution)/shard_map/rh,rd->hd/dot_general | solution.py:64
  365.0 0.8 copy.18
  (17 shorter events, 0.1 us)
Async XLA Ops:
  7.2 2.2 copy-start
  12.0 71.6 %copy-start.5 = (bf16[1,512,448]{1,2,0:T(8,128)(2,1)S(1)}, bf16[1,512,448]{1,2,0:T(8,128)(2,1)}, u32[]{:S(2)}) copy-start(bf16[1,512,448]{1,2,0:T(8,128)(2,1)} %param.16) | copy-start | bytes 1376260
  12.0 71.6 %copy-start.6 = (bf16[1,512,448]{1,2,0:T(8,128)(2,1)S(1)}, bf16[1,512,448]{1,2,0:T(8,128)(2,1)}, u32[]{:S(2)}) copy-start(bf16[1,512,448]{1,2,0:T(8,128)(2,1)} %param.15) | copy-start | bytes 1376260
  12.0 71.6 %all-to-all-start = ((bf16[32,16,4096]{2,1,0:T(8,128)(2,1)}), bf16[32,16,4096]{2,1,0:T(8,128)(2,1)}, u32[]{:S(2)}, u32[]{:S(2)}) async-start(bf16[32,16,4096]{2,1,0:T(8,128)(2,1)} %bitcast.89), calls=%async_computation | async-start | bytes 8388608 | tf_op jit(solution)/shard_map/all_to_all | solution.py:46
  23.5 310.5 %reduce-scatter.2.cloned.1.call-start = ((), (), s32[]{:S(2)}) async-start(), calls=%async_computation.3 | async-start | bytes 8650752 | tf_op jit(solution)/shard_map/reduce_scatter | solution.py:79
  83.7 5.7 %copy-start.2 = (bf16[1,4096,448]{1,2,0:T(8,128)(2,1)S(1)}, bf16[1,4096,448]{1,2,0:T(8,128)(2,1)}, u32[]{:S(2)}) copy-start(bf16[1,4096,448]{1,2,0:T(8,128)(2,1)} %param.17) | copy-start | bytes 11010052
  89.4 2.4 copy-start.4
  107.3 1.0 copy-start.3
  334.0 31.8 %copy-start.1 = (bf16[1,64,4096]{2,1,0:T(8,128)(2,1)S(1)}, bf16[1,64,4096]{2,1,0:T(8,128)(2,1)}, u32[]{:S(2)}) copy-start(bf16[1,64,4096]{2,1,0:T(8,128)(2,1)} %param.11) | copy-start | bytes 1572868
  335.6 29.4 %collective-permute-start = (bf16[64,4096]{1,0:T(8,128)(2,1)S(1)}, bf16[64,4096]{1,0:T(8,128)(2,1)S(1)}, u32[]{:S(2)}, u32[]{:S(2)}) collective-permute-start(bf16[64,4096]{1,0:T(8,128)(2,1)S(1)} %convolution_convert_fusion.3), channel_id=1, source_target_pairs={{32,0},{64,32},{96,64},{33,1},{65,33},{97,65},{34,2},{66,34},{98,6... | collective-permute-start | bytes 1572872 | tf_op jit(solution)/shard_map/ppermute | solution.py:13
Sparse Core Ops, SparseCore 0:
  107.4 226.4 reduce-scatter.1
where the time goes:
time: 373 us
  waiting for transfers between devices  214 us (57%)
  blocking collectives  62.9 us (17%)
  starting transfers between devices  34.7 us (9%)
  matrix products  27 us (7%)
  other arithmetic  14.8 us (4%)
  between operations  14.2 us (4%)
  local copies, waits for them, and re-layouts  4.79 us (1%)
    reduce_scatter x1, waiting for transfers between devices, shards(): lax.psum_scatter(padded.astype(jnp.bfloat16), 'expert', scatter_dimension...  154 us
    all_to_all x1, blocking collectives, shards(): lax.all_to_all(send_inputs, 'expert', split_axis=0, concat_axis=0, tiled=...  62.9 us
    all_to_all x1, waiting for transfers between devices, shards(): lax.all_to_all(send_grads, 'expert', split_axis=0, concat_axis=0, tiled=T...  60.1 us
    ppermute x1, starting transfers between devices, from_behind(): return lax.ppermute(x, axis, pairs)  23.2 us
    all_to_all x1, starting transfers between devices, shards(): lax.all_to_all(send_grads, 'expert', split_axis=0, concat_axis=0, tiled=T...  11.4 us
    convert_element_type x1, other arithmetic, shards(): padded.astype(jnp.bfloat16)  8.39 us
  transfers between devices with their start and end apart: 3, of which 2 were waited for; matrix products, arithmetic and copies ran while one was open for 4% of the time, Pallas kernels for 0%

commit v1 on v0

v1 whole, which is shorter than its diff:
```python
import jax
import jax.numpy as jnp
from jax import lax
from jax.experimental import pallas as pl
from jax.experimental.pallas import tpu as pltpu
from jax.sharding import PartitionSpec as P

E_WIN = 2
CAP = 16
ROWS = 512
Y_OF_CHUNK = (0, 3, 1, 2)
COPIES = 80


def kernel(
    ids_ref, slots_ref, gates_ref, tok_hbm, og_hbm, sg_hbm, su_hbm, wg_hbm, wu_hbm, wd_hbm,
    rg_hbm, rt_hbm, gg_hbm, ug_hbm, hid_hbm, out_hbm,
    bg, bt, cg, ct, part, og, tok, sg, su, wg, wu, wd, acc, gg, ug, ggt, ugt, hid, res,
    rp1d, rp1b, rq1d, rq1b, rp2d, rp2b, rq2d, rq2b,
    ssem, rsem, lsem,
):
    width = bg.shape[-1]
    half_w = width // 2
    hidden_n = sg.shape[0]
    pcols, qcols = pl.ds(0, half_w), pl.ds(half_w, half_w)

    e = lax.axis_index("expert")
    y, x, z = e // 8, (e // 2) % 4, e % 2
    a = y // 2
    b = 1 - a
    p = (y + a) % 2
    q = 1 - p
    w = 1 - z
    xp, xm, xo = (x + 1) % 4, (x + 3) % 4, (x + 2) % 4

    def dev(y_, x_, z_):
        return (y_ * 4 + x_) * 2 + z_

    y_dev = dev(2 * a + 1 - y % 2, x, z)
    z_dev = dev(y, x, w)
    xp_dev = dev(y, xp, z)
    xm_dev = dev(y, xm, z)
    c_dev = dev(3 - y, x, z)

    local = []

    def fetch(src, dst):
        c = pltpu.make_async_copy(src, dst, lsem.at[len(local)])
        c.start()
        local.append(c)
        return c

    og_in = fetch(og_hbm, og)
    tok_in = fetch(tok_hbm, tok)
    sg_in = fetch(sg_hbm, sg)
    su_in = fetch(su_hbm, su)
    wd_in = fetch(wd_hbm, wd)
    wg_in = fetch(wg_hbm, wg.at[pl.ds(0, hidden_n)])
    wu_in = fetch(wu_hbm, wu.at[pl.ds(0, hidden_n)])

    barrier = pltpu.get_barrier_semaphore()
    for d in (y_dev, z_dev, xp_dev, xm_dev, c_dev):
        pl.semaphore_signal(barrier, 1, device_id={"expert": d}, device_id_type=pl.DeviceIdType.MESH)

    remote = []

    def send(src, dst, to):
        i = len(remote)
        c = pltpu.make_async_remote_copy(
            src_ref=src, dst_ref=dst, send_sem=ssem.at[i], recv_sem=rsem.at[i],
            device_id={"expert": to}, device_id_type=pl.DeviceIdType.MESH,
        )
        c.start()
        remote.append(c)
        return c

    tokens_n = og.shape[0]
    rows32 = lax.broadcasted_iota(jnp.int32, (2 * CAP, tokens_n), 0)
    pick = jnp.zeros((2 * CAP, tokens_n), jnp.float32)
    scaled = jnp.zeros((2 * CAP, tokens_n), jnp.float32)
    for k in range(2):
        chosen = ids_ref[k:k + 1, :]
        base = jnp.where(chosen == a, 0, jnp.where(chosen == b, CAP, -CAP * CAP))
        hit = rows32 == base + slots_ref[k:k + 1, :]
        weight = gates_ref[k:k + 1, :].astype(jnp.float32) * (1.0 / 256.0)
        pick += jnp.where(hit, 1.0, 0.0)
        scaled += jnp.where(hit, weight, 0.0)
    pick = pick.astype(jnp.bfloat16)
    scaled = scaled.astype(jnp.bfloat16)

    def place(sel, src, buf, other):
        step = 1024
        for c in range(0, width, step):
            rows = jnp.dot(sel, src[:, c:c + step], preferred_element_type=jnp.float32)
            rows = rows.astype(jnp.bfloat16)
            buf[p, a, x, z, :, c:c + step] = rows[:CAP]
            other[:, c:c + step] = rows[CAP:]

    og_in.wait()
    place(scaled, og, bg, cg)
    pl.semaphore_wait(barrier, 5)

    class Gather:
        def __init__(self, buf, other):
            self.buf, self.other = buf, other

        def own(self):
            buf = self.buf
            self.cross = send(self.other, buf.at[p, a, x, z], c_dev)
            self.one_a = self.one(a)

        def one(self, m):
            sp = self.buf.at[p, m, x, z, :, pcols]
            sq = self.buf.at[p, m, x, z, :, qcols]
            return (
                send(sp, sp, y_dev), send(sp, sp, z_dev),
                send(sq, sq, xp_dev), send(sq, sq, xm_dev),
            )

        def crossed(self):
            self.cross.wait_recv()
            self.one_b = self.one(b)

        def fwd1_a(self):
            for c in self.one_a:
                c.wait_recv()
            s1 = self.buf.at[q, a, x, z, :, pcols]
            s2 = self.buf.at[p, a, xm, z, :, qcols]
            self.f1a = (send(s1, s1, z_dev), send(s2, s2, xp_dev))

        def fwd1_b(self):
            for c in self.one_b:
                c.wait_recv()
            s1 = self.buf.at[p, b, x, w, :, pcols]
            s2 = self.buf.at[p, b, xp, z, :, qcols]
            self.f1b = (send(s1, s1, y_dev), send(s2, s2, xm_dev))

        def two(self, m):
            sp = self.buf.at[:, m, x, :, :, pcols]
            sq = self.buf.at[p, m, :, z, :, qcols]
            return (
                send(sp, sp, xp_dev), send(sp, sp, xm_dev),
                send(sq, sq, y_dev), send(sq, sq, z_dev),
            )

        def two_a(self):
            for c in self.f1a:
                c.wait_recv()
            self.t_a = self.two(a)

        def two_b(self):
            for c in self.f1b:
                c.wait_recv()
            self.t_b = self.two(b)

        def fwd2_a(self):
            for c in self.t_a:
                c.wait_recv()
            s1 = self.buf.at[:, a, xm, :, :, pcols]
            s2 = self.buf.at[q, a, :, z, :, qcols]
            self.f2a = (send(s1, s1, xp_dev), send(s2, s2, z_dev))

        def fwd2_b(self):
            for c in self.t_b:
                c.wait_recv()
            s1 = self.buf.at[:, b, xp, :, :, pcols]
            s2 = self.buf.at[p, b, :, w, :, qcols]
            self.f2b = (send(s1, s1, xm_dev), send(s2, s2, y_dev))

        def done(self):
            for c in self.f2a + self.f2b:
                c.wait_recv()

    g = Gather(bg, cg)
    t = Gather(bt, ct)
    g.own()
    tok_in.wait()
    place(pick, tok, bt, ct)
    t.own()
    g.crossed()
    g.fwd1_a()
    t.crossed()
    t.fwd1_a()
    g.fwd1_b()
    g.two_a()
    t.fwd1_b()
    g.two_b()

    sg_in.wait()
    su_in.wait()
    for chunk in range(4):
        src = slice(128 * Y_OF_CHUNK[chunk], 128 * Y_OF_CHUNK[chunk] + 128)
        gate = sg[:, src].astype(jnp.float32)
        up = su[:, src].astype(jnp.float32)
        sig = 1.0 / (1.0 + jnp.exp(-gate))
        hid[:, 128 * chunk:128 * chunk + 128] = (gate * sig * up).astype(jnp.bfloat16)
    hid_out = fetch(hid, hid_hbm)
    acc[...] = jnp.zeros_like(acc)
    pad = wg.shape[0] - hidden_n
    wg[hidden_n:, :] = jnp.zeros((pad, width), wg.dtype)
    wu[hidden_n:, :] = jnp.zeros((pad, width), wu.dtype)

    g.fwd2_a()
    t.two_a()
    wd_in.wait()
    g.fwd2_b()
    t.two_b()
    g.done()
    rg_out = fetch(bg, rg_hbm)

    k_step = width // 4
    for c in range(2):
        cols = slice(256 * c, 256 * c + 256)

        def hid_step(k, _, c=c, cols=cols):
            ks = pl.ds(pl.multiple_of(k * k_step, 128), k_step)
            rows = bg[c, :, :, :, :, ks].reshape(256, k_step)
            acc[:, cols] += lax.dot_general(
                wd[:, ks], rows, (((1,), (1,)), ((), ())), preferred_element_type=jnp.float32
            )
            return 0

        lax.fori_loop(0, 4, hid_step, 0)

    t.fwd2_a()
    for chunk in range(4):
        src = slice(128 * Y_OF_CHUNK[chunk], 128 * Y_OF_CHUNK[chunk] + 128)
        dst = slice(128 * chunk, 128 * chunk + 128)
        gate = sg[:, src].astype(jnp.float32)
        up = su[:, src].astype(jnp.float32)
        sig = 1.0 / (1.0 + jnp.exp(-gate))
        down = acc[:, dst]
        g_gate = down * up * sig * (1.0 + gate * (1.0 - sig))
        g_up = down * (gate * sig)
        ggt[:, dst] = g_gate.astype(jnp.bfloat16)
        ugt[:, dst] = g_up.astype(jnp.bfloat16)
        zeros = jnp.zeros((pad, 128), jnp.float32)
        gg[dst, :] = jnp.concatenate([g_gate, zeros], axis=0).T.astype(jnp.bfloat16)
        ug[dst, :] = jnp.concatenate([g_up, zeros], axis=0).T.astype(jnp.bfloat16)
    gg_out = fetch(ggt, gg_hbm)
    ug_out = fetch(ugt, ug_hbm)

    n_step = 512

    def parts(first):
        for c in range(2):

            def part_step(n, _, c=c):
                ns = pl.ds(pl.multiple_of(first + n * n_step, 128), n_step)
                rows = slice(256 * c, 256 * c + 256)
                o = jnp.dot(gg[rows, :], wg[:, ns], preferred_element_type=jnp.float32)
                o += jnp.dot(ug[rows, :], wu[:, ns], preferred_element_type=jnp.float32)
                part[c, :, :, :, :, ns] = o.astype(jnp.bfloat16).reshape(2, 4, 2, CAP, n_step)
                return 0

            lax.fori_loop(0, half_w // n_step, part_step, 0)

    f32 = jnp.float32
    bf = jnp.bfloat16

    wg_in.wait()
    wu_in.wait()
    parts(0)
    p1 = (
        send(part.at[:, a, xo, :, :, pcols], rp1d.at[0], xp_dev),
        send(part.at[:, b, xo, :, :, pcols], rp1d.at[1], xm_dev),
    )
    p1r = (
        send(part.at[:, b, xp, :, :, pcols], rp1b.at[0, 1], xp_dev),
        send(part.at[:, a, xm, :, :, pcols], rp1b.at[1, 0], xm_dev),
    )
    t.fwd2_b()
    parts(half_w)
    q1 = (
        send(part.at[q, a, :, w, :, qcols], rq1d.at[0], y_dev),
        send(part.at[q, b, :, w, :, qcols], rq1d.at[1], z_dev),
    )
    q1r = (
        send(part.at[p, b, :, w, :, qcols], rq1b.at[0, 1], z_dev),
        send(part.at[q, a, :, z, :, qcols], rq1b.at[1, 0], y_dev),
    )

    p1[0].wait_recv()
    for i in range(2):
        for j in range(2):
            part[i, a, xp, j, :, pcols] = (
                part[i, a, xp, j, :, pcols].astype(f32) + rp1d[0, i, j].astype(f32)
            ).astype(bf)
    p1s0 = send(part.at[:, a, xp, :, :, pcols], rp1b.at[0, 0], xp_dev)
    p1[1].wait_recv()
    for i in range(2):
        for j in range(2):
            part[i, b, xm, j, :, pcols] = (
                part[i, b, xm, j, :, pcols].astype(f32) + rp1d[1, i, j].astype(f32)
            ).astype(bf)
    p1s1 = send(part.at[:, b, xm, :, :, pcols], rp1b.at[1, 1], xm_dev)

    q1[0].wait_recv()
    for i in range(4):
        part[p, a, i, w, :, qcols] = (
            part[p, a, i, w, :, qcols].astype(f32) + rq1d[0, i].astype(f32)
        ).astype(bf)
    q1s0 = send(part.at[p, a, :, w, :, qcols], rq1b.at[0, 0], z_dev)
    q1[1].wait_recv()
    for i in range(4):
        part[q, b, i, z, :, qcols] = (
            part[q, b, i, z, :, qcols].astype(f32) + rq1d[1, i].astype(f32)
        ).astype(bf)
    q1s1 = send(part.at[q, b, :, z, :, qcols], rq1b.at[1, 1], y_dev)

    t.done()
    rt_out = fetch(bt, rt_hbm)

    for c in p1r + (p1s0, p1s1):
        c.wait_recv()
    for i in range(2):
        for s, m in ((0, a), (1, b)):
            for j in range(2):
                part[i, m, x, j, :, pcols] = (
                    part[i, m, x, j, :, pcols].astype(f32)
                    + rp1b[0, s, i, j].astype(f32) + rp1b[1, s, i, j].astype(f32)
                ).astype(bf)
    p2 = (
        send(part.at[q, a, x, w, :, pcols], rp2d.at[0], y_dev),
        send(part.at[q, b, x, w, :, pcols], rp2d.at[1], z_dev),
    )
    p2r = (
        send(part.at[p, b, x, w, :, pcols], rp2b.at[0, 1], z_dev),
        send(part.at[q, a, x, z, :, pcols], rp2b.at[1, 0], y_dev),
    )
    for c in q1r + (q1s0, q1s1):
        c.wait_recv()
    for i in range(4):
        for s, m in ((0, a), (1, b)):
            part[p, m, i, z, :, qcols] = (
                part[p, m, i, z, :, qcols].astype(f32)
                + rq1b[0, s, i].astype(f32) + rq1b[1, s, i].astype(f32)
            ).astype(bf)
    q2 = (
        send(part.at[p, a, xo, z, :, qcols], rq2d.at[0], xp_dev),
        send(part.at[p, b, xo, z, :, qcols], rq2d.at[1], xm_dev),
    )
    q2r = (
        send(part.at[p, b, xp, z, :, qcols], rq2b.at[0, 1], xp_dev),
        send(part.at[p, a, xm, z, :, qcols], rq2b.at[1, 0], xm_dev),
    )

    p2[0].wait_recv()
    part[p, a, x, w, :, pcols] = (
        part[p, a, x, w, :, pcols].astype(f32) + rp2d[0].astype(f32)
    ).astype(bf)
    p2s0 = send(part.at[p, a, x, w, :, pcols], rp2b.at[0, 0], z_dev)
    p2[1].wait_recv()
    part[q, b, x, z, :, pcols] = (
        part[q, b, x, z, :, pcols].astype(f32) + rp2d[1].astype(f32)
    ).astype(bf)
    p2s1 = send(part.at[q, b, x, z, :, pcols], rp2b.at[1, 1], y_dev)
    q2[0].wait_recv()
    part[p, a, xp, z, :, qcols] = (
        part[p, a, xp, z, :, qcols].astype(f32) + rq2d[0].astype(f32)
    ).astype(bf)
    q2s0 = send(part.at[p, a, xp, z, :, qcols], rq2b.at[0, 0], xp_dev)
    q2[1].wait_recv()
    part[p, b, xm, z, :, qcols] = (
        part[p, b, xm, z, :, qcols].astype(f32) + rq2d[1].astype(f32)
    ).astype(bf)
    q2s1 = send(part.at[p, b, xm, z, :, qcols], rq2b.at[1, 1], xm_dev)

    for c in p2r + (p2s0, p2s1):
        c.wait_recv()
    for s, m in ((0, a), (1, b)):
        res[s, :, pcols] = (
            part[p, m, x, z, :, pcols].astype(f32)
            + rp2b[0, s].astype(f32) + rp2b[1, s].astype(f32)
        ).astype(bf)
    for c in q2r + (q2s0, q2s1):
        c.wait_recv()
    for s, m in ((0, a), (1, b)):
        res[s, :, qcols] = (
            part[p, m, x, z, :, qcols].astype(f32)
            + rq2b[0, s].astype(f32) + rq2b[1, s].astype(f32)
        ).astype(bf)
    res_out = fetch(res, out_hbm)

    for c in remote:
        c.wait_send()
    for c in (hid_out, rg_out, gg_out, ug_out, rt_out, res_out):
        c.wait()


def exchange(ids, slots, gates, tok, og, sg, su, wg, wu, wd):
    width = tok.shape[-1]
    tokens_n = tok.shape[0]
    hidden_n = sg.shape[0]
    half = width // 2
    bf = jnp.bfloat16
    rows_shape = (2, 2, 4, 2, CAP, width)
    padded = -(-hidden_n // 128) * 128
    any_spec = pl.BlockSpec(memory_space=pl.ANY)
    vmem_spec = pl.BlockSpec(memory_space=pltpu.VMEM)
    vm = pltpu.VMEM
    return pl.pallas_call(
        kernel,
        name="exchange",
        out_shape=(
            jax.ShapeDtypeStruct(rows_shape, bf),
            jax.ShapeDtypeStruct(rows_shape, bf),
            jax.ShapeDtypeStruct((hidden_n, ROWS), bf),
            jax.ShapeDtypeStruct((hidden_n, ROWS), bf),
            jax.ShapeDtypeStruct((hidden_n, ROWS), bf),
            jax.ShapeDtypeStruct((2, CAP, width), bf),
        ),
        in_specs=[vmem_spec] * 3 + [any_spec] * 7,
        out_specs=[any_spec] * 6,
        scratch_shapes=[
            vm(rows_shape, bf), vm(rows_shape, bf),
            vm((CAP, width), bf), vm((CAP, width), bf),
            vm(rows_shape, bf),
            vm((tokens_n, width), bf), vm((tokens_n, width), bf),
            vm((hidden_n, ROWS), bf), vm((hidden_n, ROWS), bf),
            vm((padded, width), bf), vm((padded, width), bf), vm((hidden_n, width), bf),
            vm((hidden_n, ROWS), jnp.float32),
            vm((ROWS, padded), bf), vm((ROWS, padded), bf),
            vm((hidden_n, ROWS), bf), vm((hidden_n, ROWS), bf), vm((hidden_n, ROWS), bf),
            vm((2, CAP, width), bf),
            vm((2, 2, 2, CAP, half), bf), vm((2, 2, 2, 2, CAP, half), bf),
            vm((2, 4, CAP, half), bf), vm((2, 2, 4, CAP, half), bf),
            vm((2, CAP, half), bf), vm((2, 2, CAP, half), bf),
            vm((2, CAP, half), bf), vm((2, 2, CAP, half), bf),
            pltpu.SemaphoreType.DMA((COPIES,)), pltpu.SemaphoreType.DMA((COPIES,)),
            pltpu.SemaphoreType.DMA((16,)),
        ],
        compiler_params=pltpu.CompilerParams(
            collective_id=0, has_side_effects=True, vmem_limit_bytes=56 << 20
        ),
        cost_estimate=pl.CostEstimate(
            flops=6 * ROWS * hidden_n * width, transcendentals=2 * ROWS * hidden_n,
            bytes_accessed=40 << 20,
        ),
    )(ids, slots, gates, tok, og, sg, su, wg, wu, wd)


def shards(
    tokens, out_grad, expert_ids, slot_ids, gate_int, saved_gate, saved_up, w_gate, w_up, w_down
):
    width = tokens.shape[-1]
    sections = lax.axis_size("section")
    devices = lax.axis_size("expert")
    ids, slots, gates = expert_ids[0].T, slot_ids[0].T, gate_int[0].T

    back = [(s * devices + i, (s - 1) * devices + i) for s in range(1, sections) for i in range(devices)]
    back_cross = [
        (s * devices + i, (s - 1) * devices + (3 - i // 8) * 8 + i % 8)
        for s in range(1, sections) for i in range(devices)
    ]
    axes = ("section", "expert")
    table = lax.ppermute(jnp.stack([ids, slots]), axes, back)

    rows_grad, rows_in, gate_t, up_t, hidden_t, summed = exchange(
        ids, slots, gates, tokens[0], out_grad[0], saved_gate[0].T, saved_up[0].T,
        w_gate[0].T, w_up[0].T, w_down[0],
    )
    own = lax.ppermute(summed[0], axes, back)
    other = lax.ppermute(summed[1], axes, back_cross)

    rows_grad = rows_grad.reshape(ROWS, width)
    rows_in = rows_in.reshape(ROWS, width)

    def product(left, right):
        return jnp.dot(left, right, preferred_element_type=jnp.float32).astype(jnp.bfloat16)

    grad_down = product(hidden_t, rows_grad)
    grad_gate = product(gate_t, rows_in).T
    grad_up = product(up_t, rows_in).T

    mine = lax.axis_index("expert") // (devices // E_WIN)
    slot = lax.iota(jnp.int32, CAP)

    def taken(expert):
        hit = jnp.logical_and(table[0][:, :, None] == expert, table[1][:, :, None] == slot)
        return jnp.any(hit, axis=0)

    select = jnp.concatenate([taken(mine), taken(1 - mine)], axis=1).astype(jnp.bfloat16)
    arriving = jnp.dot(
        select, jnp.concatenate([own, other], axis=0), preferred_element_type=jnp.float32
    ).astype(jnp.bfloat16)
    return (arriving[None], grad_gate[None], grad_up[None], grad_down[None])


def solution(mesh):
    row = P("section", "expert", None)
    col = P("section", None, "expert")
    return jax.shard_map(
        shards,
        mesh=mesh,
        in_specs=(row,) * 5 + (col,) * 4 + (row,),
        out_specs=(row, col, col, row),
        check_vma=False,
    )
```

time: 373 us -> 112 us (0.30)
  waiting for transfers between devices: 214 us -> 0.01 us
  Pallas kernels: 0 us -> 83.4 us
  blocking collectives: 62.9 us -> 0 us
  starting transfers between devices: 34.7 us -> 10.4 us
  other arithmetic: 14.8 us -> 0.72 us
  between operations: 14.2 us -> 0.73 us
  matrix products: 27 us -> 15.4 us
  local copies, waits for them, and re-layouts: 4.79 us -> 1 us
    reduce_scatter x1 -> x0, waiting for transfers between devices: 154 us -> none  [shards(): lax.psum_scatter(padded.astype(jnp.bfloat16), 'expert', scatter_dimension...]
    pallas_call x0 -> x1, Pallas kernels: none -> 83.4 us  [exchange(): pl.pallas_call(kernel, name='exchange', out_shape=(jax.ShapeDtypeStruct(r...]
    all_to_all x1 -> x0, blocking collectives: 62.9 us -> none  [shards(): lax.all_to_all(send_inputs, 'expert', split_axis=0, concat_axis=0, tiled=...]
    all_to_all x1 -> x0, waiting for transfers between devices: 60.1 us -> none  [shards(): lax.all_to_all(send_grads, 'expert', split_axis=0, concat_axis=0, tiled=T...]
    ppermute x1 -> x3, starting transfers between devices: 23.2 us -> 10.4 us  [the longest x1 5.08 us: shards(): own = lax.ppermute(summed[0], axes, back)]
    dot_general x9 -> x4, matrix products: 27 us -> 15.4 us  [the longest x3 14.2 us: product(): jnp.dot(left, right, preferred_element_type=jnp.float32)]
    all_to_all x1 -> x0, starting transfers between devices: 11.4 us -> none  [shards(): lax.all_to_all(send_grads, 'expert', split_axis=0, concat_axis=0, tiled=T...]
    convert_element_type x2 -> x0, other arithmetic: 8.39 us -> none  [the longest x1 8.39 us: shards(): padded.astype(jnp.bfloat16)]
  transfers between devices with their start and end apart: 3 -> 3, of which waited for: 2 -> 0; matrix products, arithmetic and copies ran while one was open for 4% -> 14% of each run, Pallas kernels for 0% -> 75%
where the time goes in v1:
time: 112 us
  Pallas kernels  83.4 us (74%)
  matrix products  15.4 us (14%)
  starting transfers between devices  10.4 us (9%)
    pallas_call x1, Pallas kernels, exchange(): pl.pallas_call(kernel, name='exchange', out_shape=(jax.ShapeDtypeStruct(r...  83.4 us
    dot_general x3, matrix products, product(): jnp.dot(left, right, preferred_element_type=jnp.float32)  14.2 us
    ppermute x1, starting transfers between devices, shards(): own = lax.ppermute(summed[0], axes, back)  5.08 us
    ppermute x1, starting transfers between devices, shards(): table = lax.ppermute(jnp.stack([ids, slots]), axes, back)  3.32 us
  transfers between devices with their start and end apart: 3, of which 0 were waited for; matrix products, arithmetic and copies ran while one was open for 14% of the time, Pallas kernels for 75%

profile of v1, /device:TPU:1, one launch (start us, length us, event | category | flops | bytes accessed | tf_op | source)
XLA Modules:
  0.0 111.7 jit_solution(3961950775229471702)
XLA Ops:
  0.6 0.7 pad_add_fusion
  1.3 3.3 %collective-permute-start = (s32[2,2,64]{2,1,0:T(2,128)S(1)}, s32[2,2,64]{2,1,0:T(2,128)S(1)}, u32[]{:S(2)}, u32[]{:S(2)}) collective-permute-start(s32[2,2,64]{2,1,0:T(2,128)S(1)} %pad_add_fusion), channel_id=1, source_target_pairs={{32,0},{33,1},{34,2},{35,3},{36,4},{37,5},{38,6},{39,7},{40,8},{41... | collective-permute-start | bytes 3080 | tf_op jit(solution)/shard_map/ppermute | solution.py:457
  4.7 83.4 %exchange.1 = (bf16[2,2,4,2,16,4096]{5,4,3,2,1,0:T(8,128)(2,1)}, bf16[2,2,4,2,16,4096]{5,4,3,2,1,0:T(8,128)(2,1)}, bf16[448,512]{1,0:T(8,128)(2,1)}, bf16[448,51...) custom-call(s32[2,64]{1,0:T(2,128)} %bitcast.55, s32[2,64]{1,0:T(2,128)} %bitcast.57, ...), custom_call_target="tpu_custom_call" | custom-call | flops 5637144576 | bytes 41943040 | tf_op jit(solution)/shard_map/exchange/pallas_call | solution.py:402
  88.1 1.0 slice_bitcast_fusion.1
  89.1 5.1 %collective-permute-start.1 = (bf16[16,4096]{1,0:T(8,128)(2,1)S(1)}, bf16[16,4096]{1,0:T(8,128)(2,1)S(1)}, u32[]{:S(2)}, u32[]{:S(2)}) collective-permute-start(bf16[16,4096]{1,0:T(8,128)(2,1)S(1)} %get-tuple-element.18), channel_id=1, source_target_pairs={{32,0},{33,1},{34,2},{35,3},{36,4},{37,5},{38,6},{39,7},{40,8},{41... | collective-permute-start | bytes 393224 | tf_op jit(solution)/shard_map/ppermute | solution.py:463
  94.2 2.0 %collective-permute-start.2 = (bf16[16,4096]{1,0:T(8,128)(2,1)S(1)}, bf16[16,4096]{1,0:T(8,128)(2,1)S(1)}, u32[]{:S(2)}, u32[]{:S(2)}) collective-permute-start(bf16[16,4096]{1,0:T(8,128)(2,1)S(1)} %get-tuple-element.19), channel_id=1, source_target_pairs={{32,24},{33,25},{34,26},{35,27},{36,28},{37,29},{38,30},{39,31},{4... | collective-permute-start | bytes 393224 | tf_op jit(solution)/shard_map/ppermute | solution.py:464
  96.2 0.0 copy-start.1
  96.2 0.0 copy-start.3
  96.2 6.4 %fusion.1 = bf16[1,4096,448]{1,2,0:T(8,128)(2,1)} fusion(bf16[448,512]{1,0:T(8,128)(2,1)} %get-tuple-element.12, bf16[512,4096]{1,0:T(8,128)(2,1)} %bitcast.67), kind=kOutput, calls=%fused_computation.4 | convolution fusion | flops 1880883200 | bytes 8323072 | tf_op jit(solution)/shard_map/dot_general | solution.py:470
  102.6 0.0 copy-done.1
  102.6 0.0 copy-done.3
  102.6 0.0 copy-start
  102.6 0.0 copy-start.2
  102.6 3.9 %fusion.2 = bf16[1,4096,448]{1,2,0:T(8,128)(2,1)} fusion(bf16[448,512]{1,0:T(8,128)(2,1)S(1)} %copy-done.3, bf16[512,4096]{1,0:T(8,128)(2,1)S(1)} %bitcast.68), kind=kOutput, calls=%fused_computation.5 | convolution fusion | flops 1880883200 | bytes 8323072 | tf_op jit(solution)/shard_map/dot_general | solution.py:470
  106.6 0.0 copy-done
  106.6 0.0 copy-done.2
  106.6 3.9 %fusion = bf16[1,448,4096]{2,1,0:T(8,128)(2,1)} fusion(bf16[448,512]{1,0:T(8,128)(2,1)S(1)} %copy-done.2, bf16[512,4096]{1,0:T(8,128)(2,1)S(1)} %bitcast.66), kind=kOutput, calls=%fused_computation.3 | convolution fusion | flops 1880883200 | bytes 8323072 | tf_op jit(solution)/shard_map/dot_general | solution.py:470
  110.5 0.0 collective-permute-done
  110.5 0.0 collective-permute-done.1
  110.5 0.0 collective-permute-done.2
  110.5 1.1 %fusion.3 = bf16[1,64,4096]{2,1,0:T(8,128)(2,1)} fusion(bf16[16,4096]{1,0:T(8,128)(2,1)S(1)} %collective-permute-done.2, bf16[16,4096]{1,0:T(8,128)(2,1)S(1)} %collective-permute-done.1, pred[64,16]{0,1:T(8,128)(4,1)S(1)} %get-tuple-element.17, pred[64,16]{0,1:T(8,128)(4,1)S(1)} %get-tuple-element.16), kind=kOutput, calls=%fused_computation.7 | convolution fusion | flops 17565696 | bytes 788480 | tf_op jit(solution)/shard_map/dot_general | solution.py:484
  (3 shorter events, 0.0 us)
Async XLA Ops:
  1.3 109.2 %collective-permute-start = (s32[2,2,64]{2,1,0:T(2,128)S(1)}, s32[2,2,64]{2,1,0:T(2,128)S(1)}, u32[]{:S(2)}, u32[]{:S(2)}) collective-permute-start(s32[2,2,64]{2,1,0:T(2,128)S(1)} %pad_add_fusion), channel_id=1, source_target_pairs={{32,0},{33,1},{34,2},{35,3},{36,4},{37,5},{38,6},{39,7},{40,8},{41... | collective-permute-start | bytes 3080 | tf_op jit(solution)/shard_map/ppermute | solution.py:457
  89.1 21.4 %collective-permute-start.1 = (bf16[16,4096]{1,0:T(8,128)(2,1)S(1)}, bf16[16,4096]{1,0:T(8,128)(2,1)S(1)}, u32[]{:S(2)}, u32[]{:S(2)}) collective-permute-start(bf16[16,4096]{1,0:T(8,128)(2,1)S(1)} %get-tuple-element.18), channel_id=1, source_target_pairs={{32,0},{33,1},{34,2},{35,3},{36,4},{37,5},{38,6},{39,7},{40,8},{41... | collective-permute-start | bytes 393224 | tf_op jit(solution)/shard_map/ppermute | solution.py:463
  94.2 16.3 %collective-permute-start.2 = (bf16[16,4096]{1,0:T(8,128)(2,1)S(1)}, bf16[16,4096]{1,0:T(8,128)(2,1)S(1)}, u32[]{:S(2)}, u32[]{:S(2)}) collective-permute-start(bf16[16,4096]{1,0:T(8,128)(2,1)S(1)} %get-tuple-element.19), channel_id=1, source_target_pairs={{32,24},{33,25},{34,26},{35,27},{36,28},{37,29},{38,30},{39,31},{4... | collective-permute-start | bytes 393224 | tf_op jit(solution)/shard_map/ppermute | solution.py:464
  96.2 6.4 %copy-start.1 = (bf16[2,2,4,2,16,4096]{5,4,3,2,1,0:T(8,128)(2,1)S(1)}, bf16[2,2,4,2,16,4096]{5,4,3,2,1,0:T(8,128)(2,1)}, u32[]{:S(2)}) copy-start(bf16[2,2,4,2,16,4096]{5,4,3,2,1,0:T(8,128)(2,1)} %get-tuple-element.11) | copy-start | bytes 12582916
  96.2 6.4 %copy-start.3 = (bf16[448,512]{1,0:T(8,128)(2,1)S(1)}, bf16[448,512]{1,0:T(8,128)(2,1)}, u32[]{:S(2)}) copy-start(bf16[448,512]{1,0:T(8,128)(2,1)} %get-tuple-element.13) | copy-start | bytes 1376260
  102.6 3.9 %copy-start = (bf16[2,2,4,2,16,4096]{5,4,3,2,1,0:T(8,128)(2,1)S(1)}, bf16[2,2,4,2,16,4096]{5,4,3,2,1,0:T(8,128)(2,1)}, u32[]{:S(2)}) copy-start(bf16[2,2,4,2,16,4096]{5,4,3,2,1,0:T(8,128)(2,1)} %get-tuple-element.15) | copy-start | bytes 12582916
  102.6 3.9 %copy-start.2 = (bf16[448,512]{1,0:T(8,128)(2,1)S(1)}, bf16[448,512]{1,0:T(8,128)(2,1)}, u32[]{:S(2)}) copy-start(bf16[448,512]{1,0:T(8,128)(2,1)} %get-tuple-element.14) | copy-start | bytes 1376260

commit v2 on v1

v2 whole, which is shorter than its diff:
```python
import jax
import jax.numpy as jnp
from jax import lax
from jax.experimental import pallas as pl
from jax.experimental.pallas import tpu as pltpu
from jax.sharding import PartitionSpec as P

CAP = 16
ROWS = 512
Y_OF_CHUNK = (0, 3, 1, 2)
COPIES = 112
PIECES = 2
VMEM_MIB = 40


def kernel(
    ids_hbm, slots_hbm, gates_hbm, tok_hbm, og_hbm, sg_hbm, su_hbm, wg_hbm, wu_hbm, wd_hbm,
    arr_hbm, dg_hbm, du_hbm, dd_hbm,
    bg, bt, cg, ct, part, og, tok, sg, su, wg, wu, wd, acc, fa, fb, gg, ug, ggt, ugt, hid,
    res, fin, pick_out, pick_in, ids_ref, slots_ref, gates_ref,
    rp1d, rp1b, rq1d, rq1b, rp2d, rp2b, rq2d, rq2b,
    ssem, rsem, lsem,
):
    f32 = jnp.float32
    bf = jnp.bfloat16
    width = bg.shape[-1]
    half_w = width // 2
    piece = half_w // PIECES
    hidden_n = sg.shape[0]
    pad = wg.shape[0] - hidden_n
    pcols, qcols = pl.ds(0, half_w), pl.ds(half_w, half_w)

    sections = lax.axis_size("section")
    sec = lax.axis_index("section")
    e = lax.axis_index("expert")
    y, x, z = e // 8, (e // 2) % 4, e % 2
    a = y // 2
    b = 1 - a
    p = (y + a) % 2
    q = 1 - p
    w = 1 - z
    xp, xm, xo = (x + 1) % 4, (x + 3) % 4, (x + 2) % 4
    before, after = (sec + sections - 1) % sections, (sec + 1) % sections

    def dev(y_, x_, z_):
        return (y_ * 4 + x_) * 2 + z_

    cross = dev(3 - y, x, z)
    y_dev = (sec, dev(2 * a + 1 - y % 2, x, z))
    z_dev = (sec, dev(y, x, w))
    xp_dev = (sec, dev(y, xp, z))
    xm_dev = (sec, dev(y, xm, z))
    c_dev = (sec, cross)

    local = []

    def fetch(src, dst):
        c = pltpu.make_async_copy(src, dst, lsem.at[len(local)])
        c.start()
        local.append(c)
        return c

    small_in = (fetch(ids_hbm, ids_ref), fetch(slots_hbm, slots_ref), fetch(gates_hbm, gates_ref))
    og_in = fetch(og_hbm, og)
    tok_in = fetch(tok_hbm, tok)
    sg_in = fetch(sg_hbm, sg)
    su_in = fetch(su_hbm, su)
    wd_in = fetch(wd_hbm, wd.at[pl.ds(0, hidden_n)])
    wg_in = fetch(wg_hbm, wg.at[pl.ds(0, hidden_n)])
    wu_in = fetch(wu_hbm, wu.at[pl.ds(0, hidden_n)])

    barrier = pltpu.get_barrier_semaphore()
    for d in (y_dev, z_dev, xp_dev, xm_dev, c_dev, (after, e), (after, cross)):
        pl.semaphore_signal(barrier, 1, device_id=d, device_id_type=pl.DeviceIdType.MESH)

    remote = []

    def send(src, dst, to):
        i = len(remote)
        c = pltpu.make_async_remote_copy(
            src_ref=src, dst_ref=dst, send_sem=ssem.at[i], recv_sem=rsem.at[i],
            device_id=to, device_id_type=pl.DeviceIdType.MESH,
        )
        c.start()
        remote.append(c)
        return c

    def arrived(copies):
        for c in copies:
            c.wait_recv()

    for c in small_in:
        c.wait()
    tokens_n = og.shape[0]
    rows32 = lax.broadcasted_iota(jnp.int32, (2 * CAP, tokens_n), 0)
    pick = jnp.zeros((2 * CAP, tokens_n), f32)
    scaled = jnp.zeros((2 * CAP, tokens_n), f32)
    for k in range(2):
        chosen = ids_ref[k:k + 1, :]
        base = jnp.where(chosen == a, 0, jnp.where(chosen == b, CAP, -CAP * CAP))
        hit = rows32 == base + slots_ref[k:k + 1, :]
        weight = gates_ref[k:k + 1, :].astype(f32) * (1.0 / 256.0)
        pick += jnp.where(hit, 1.0, 0.0)
        scaled += jnp.where(hit, weight, 0.0)
    pick = pick.astype(bf)
    scaled = scaled.astype(bf)
    pick_out[...] = pick

    def place(sel, src, buf, other):
        step = 1024
        for c in range(0, width, step):
            rows = jnp.dot(sel, src[:, c:c + step], preferred_element_type=f32)
            rows = rows.astype(bf)
            buf[p, a, x, z, :, c:c + step] = rows[:CAP]
            other[:, c:c + step] = rows[CAP:]

    og_in.wait()
    place(scaled, og, bg, cg)
    pl.semaphore_wait(barrier, 7)

    class Gather:
        def __init__(self, buf, other):
            self.buf, self.other = buf, other

        def own(self):
            buf = self.buf
            self.cross = send(self.other, buf.at[p, a, x, z], c_dev)
            self.one_a = self.one(a)

        def one(self, m):
            sp = self.buf.at[p, m, x, z, :, pcols]
            sq = self.buf.at[p, m, x, z, :, qcols]
            return (
                send(sp, sp, y_dev), send(sp, sp, z_dev),
                send(sq, sq, xp_dev), send(sq, sq, xm_dev),
            )

        def crossed(self):
            self.cross.wait_recv()
            self.one_b = self.one(b)

        def fwd1_a(self):
            arrived(self.one_a)
            s1 = self.buf.at[q, a, x, z, :, pcols]
            s2 = self.buf.at[p, a, xm, z, :, qcols]
            self.f1a = (send(s1, s1, z_dev), send(s2, s2, xp_dev))

        def fwd1_b(self):
            arrived(self.one_b)
            s1 = self.buf.at[p, b, x, w, :, pcols]
            s2 = self.buf.at[p, b, xp, z, :, qcols]
            self.f1b = (send(s1, s1, y_dev), send(s2, s2, xm_dev))

        def two(self, m):
            sp = self.buf.at[:, m, x, :, :, pcols]
            sq = self.buf.at[p, m, :, z, :, qcols]
            return (
                send(sp, sp, xp_dev), send(sp, sp, xm_dev),
                send(sq, sq, y_dev), send(sq, sq, z_dev),
            )

        def two_a(self):
            arrived(self.f1a)
            self.t_a = self.two(a)

        def two_b(self):
            arrived(self.f1b)
            self.t_b = self.two(b)

        def fwd2_a(self):
            arrived(self.t_a)
            s1 = self.buf.at[:, a, xm, :, :, pcols]
            s2 = self.buf.at[q, a, :, z, :, qcols]
            self.f2a = (send(s1, s1, xp_dev), send(s2, s2, z_dev))

        def fwd2_b(self):
            arrived(self.t_b)
            s1 = self.buf.at[:, b, xp, :, :, pcols]
            s2 = self.buf.at[p, b, :, w, :, qcols]
            self.f2b = (send(s1, s1, xm_dev), send(s2, s2, y_dev))

        def done(self):
            arrived(self.f2a + self.f2b)

    g = Gather(bg, cg)
    t = Gather(bt, ct)
    g.own()
    tok_in.wait()
    place(pick, tok, bt, ct)
    t.own()
    g.crossed()
    g.fwd1_a()
    t.crossed()
    t.fwd1_a()
    g.fwd1_b()
    g.two_a()
    t.fwd1_b()
    g.two_b()

    pick_sent = send(pick_out, pick_in, (before, e))

    sg_in.wait()
    su_in.wait()
    zeros = jnp.zeros((pad, 128), f32)
    for chunk in range(4):
        src = slice(128 * Y_OF_CHUNK[chunk], 128 * Y_OF_CHUNK[chunk] + 128)
        dst = slice(128 * chunk, 128 * chunk + 128)
        gate = sg[:, src].astype(f32)
        up = su[:, src].astype(f32)
        sig = 1.0 / (1.0 + jnp.exp(-gate))
        active = gate * sig
        hid[:, dst] = (active * up).astype(bf)
        slope = up * sig * (1.0 + gate * (1.0 - sig))
        fa[dst, :] = jnp.concatenate([slope, zeros], axis=0).T
        fb[dst, :] = jnp.concatenate([active, zeros], axis=0).T
    acc[...] = jnp.zeros_like(acc)
    for buf in (wd, wg, wu):
        buf[hidden_n:, :] = jnp.zeros((pad, width), bf)

    g.fwd2_a()
    t.two_a()
    wd_in.wait()
    g.fwd2_b()
    t.two_b()
    g.done()

    k_step = width // 4

    def hid_step(k, _):
        ks = pl.ds(pl.multiple_of(k * k_step, 128), k_step)
        rows = bg[:, :, :, :, :, ks].reshape(ROWS, k_step)
        acc[...] += lax.dot_general(
            rows, wd[:, ks], (((1,), (1,)), ((), ())), preferred_element_type=f32
        )
        return 0

    lax.fori_loop(0, 4, hid_step, 0)
    gg[...] = (acc[...] * fa[...]).astype(bf)
    ug[...] = (acc[...] * fb[...]).astype(bf)

    n_step = 512

    def parts(first):

        def part_step(n, _):
            ns = pl.ds(pl.multiple_of(first + n * n_step, 128), n_step)
            o = jnp.dot(gg[...], wg[:, ns], preferred_element_type=f32)
            o += jnp.dot(ug[...], wu[:, ns], preferred_element_type=f32)
            part[:, :, :, :, :, ns] = o.astype(bf).reshape(2, 2, 4, 2, CAP, n_step)
            return 0

        lax.fori_loop(0, piece // n_step, part_step, 0)

    def plus(dst, index, *others):
        total = dst[index].astype(f32)
        for o in others:
            total += o.astype(f32)
        dst[index] = total.astype(bf)

    def to_before(c):
        self_cols = c
        return (
            send(res.at[0, :, self_cols], fin.at[0, :, self_cols], (before, e)),
            send(res.at[1, :, self_cols], fin.at[1, :, self_cols], (before, cross)),
        )

    class ScatterP:
        def __init__(self, k):
            self.k, self.first = k, k * piece
            self.c = pl.ds(self.first, piece)

        def start(self):
            k, c = self.k, self.c
            parts(self.first)
            self.d1 = (
                send(part.at[:, a, xo, :, :, c], rp1d.at[k, 0], xp_dev),
                send(part.at[:, b, xo, :, :, c], rp1d.at[k, 1], xm_dev),
            )
            self.b1 = (
                send(part.at[:, b, xp, :, :, c], rp1b.at[k, 0, 1], xp_dev),
                send(part.at[:, a, xm, :, :, c], rp1b.at[k, 1, 0], xm_dev),
            )

        def diag1(self):
            k, c = self.k, self.c
            arrived(self.d1[:1])
            for i in range(2):
                for j in range(2):
                    plus(part, (i, a, xp, j, slice(None), c), rp1d[k, 0, i, j])
            s0 = send(part.at[:, a, xp, :, :, c], rp1b.at[k, 0, 0], xp_dev)
            arrived(self.d1[1:])
            for i in range(2):
                for j in range(2):
                    plus(part, (i, b, xm, j, slice(None), c), rp1d[k, 1, i, j])
            s1 = send(part.at[:, b, xm, :, :, c], rp1b.at[k, 1, 1], xm_dev)
            self.b1 += (s0, s1)

        def sum1(self):
            k, c = self.k, self.c
            arrived(self.b1)
            for i in range(2):
                for s, m in ((0, a), (1, b)):
                    for j in range(2):
                        plus(part, (i, m, x, j, slice(None), c), rp1b[k, 0, s, i, j], rp1b[k, 1, s, i, j])
            self.d2 = (
                send(part.at[q, a, x, w, :, c], rp2d.at[k, 0], y_dev),
                send(part.at[q, b, x, w, :, c], rp2d.at[k, 1], z_dev),
            )
            self.b2 = (
                send(part.at[p, b, x, w, :, c], rp2b.at[k, 0, 1], z_dev),
                send(part.at[q, a, x, z, :, c], rp2b.at[k, 1, 0], y_dev),
            )

        def diag2(self):
            k, c = self.k, self.c
            arrived(self.d2[:1])
            plus(part, (p, a, x, w, slice(None), c), rp2d[k, 0])
            s0 = send(part.at[p, a, x, w, :, c], rp2b.at[k, 0, 0], z_dev)
            arrived(self.d2[1:])
            plus(part, (q, b, x, z, slice(None), c), rp2d[k, 1])
            s1 = send(part.at[q, b, x, z, :, c], rp2b.at[k, 1, 1], y_dev)
            self.b2 += (s0, s1)

        def last(self):
            k, c = self.k, self.c
            arrived(self.b2)
            for s, m in ((0, a), (1, b)):
                res[s, :, c] = (
                    part[p, m, x, z, :, c].astype(f32)
                    + rp2b[k, 0, s].astype(f32) + rp2b[k, 1, s].astype(f32)
                ).astype(bf)
            self.out = to_before(c)

    class ScatterQ:
        def __init__(self, k):
            self.k, self.first = k, half_w + k * piece
            self.c = pl.ds(self.first, piece)

        def start(self):
            k, c = self.k, self.c
            parts(self.first)
            self.d1 = (
                send(part.at[q, a, :, w, :, c], rq1d.at[k, 0], y_dev),
                send(part.at[q, b, :, w, :, c], rq1d.at[k, 1], z_dev),
            )
            self.b1 = (
                send(part.at[p, b, :, w, :, c], rq1b.at[k, 0, 1], z_dev),
                send(part.at[q, a, :, z, :, c], rq1b.at[k, 1, 0], y_dev),
            )

        def diag1(self):
            k, c = self.k, self.c
            arrived(self.d1[:1])
            for i in range(4):
                plus(part, (p, a, i, w, slice(None), c), rq1d[k, 0, i])
            s0 = send(part.at[p, a, :, w, :, c], rq1b.at[k, 0, 0], z_dev)
            arrived(self.d1[1:])
            for i in range(4):
                plus(part, (q, b, i, z, slice(None), c), rq1d[k, 1, i])
            s1 = send(part.at[q, b, :, z, :, c], rq1b.at[k, 1, 1], y_dev)
            self.b1 += (s0, s1)

        def sum1(self):
            k, c = self.k, self.c
            arrived(self.b1)
            for i in range(4):
                for s, m in ((0, a), (1, b)):
                    plus(part, (p, m, i, z, slice(None), c), rq1b[k, 0, s, i], rq1b[k, 1, s, i])
            self.d2 = (
                send(part.at[p, a, xo, z, :, c], rq2d.at[k, 0], xp_dev),
                send(part.at[p, b, xo, z, :, c], rq2d.at[k, 1], xm_dev),
            )
            self.b2 = (
                send(part.at[p, b, xp, z, :, c], rq2b.at[k, 0, 1], xp_dev),
                send(part.at[p, a, xm, z, :, c], rq2b.at[k, 1, 0], xm_dev),
            )

        def diag2(self):
            k, c = self.k, self.c
            arrived(self.d2[:1])
            plus(part, (p, a, xp, z, slice(None), c), rq2d[k, 0])
            s0 = send(part.at[p, a, xp, z, :, c], rq2b.at[k, 0, 0], xp_dev)
            arrived(self.d2[1:])
            plus(part, (p, b, xm, z, slice(None), c), rq2d[k, 1])
            s1 = send(part.at[p, b, xm, z, :, c], rq2b.at[k, 1, 1], xm_dev)
            self.b2 += (s0, s1)

        def last(self):
            k, c = self.k, self.c
            arrived(self.b2)
            for s, m in ((0, a), (1, b)):
                res[s, :, c] = (
                    part[p, m, x, z, :, c].astype(f32)
                    + rq2b[k, 0, s].astype(f32) + rq2b[k, 1, s].astype(f32)
                ).astype(bf)
            self.out = to_before(c)

    def weight_grad(left, rows, out):

        def grad_step(n, _):
            ns = pl.ds(pl.multiple_of(n * n_step, 128), n_step)
            right = rows[:, :, :, :, :, ns].reshape(ROWS, n_step)
            out[pl.ds(0, hidden_n), ns] = jnp.dot(left[...], right, preferred_element_type=f32).astype(bf)
            return 0

        lax.fori_loop(0, width // n_step, grad_step, 0)

    p0, p1 = ScatterP(0), ScatterP(1)
    q0, q1 = ScatterQ(0), ScatterQ(1)
    wg_in.wait()
    wu_in.wait()
    p0.start()
    q0.start()
    p1.start()
    q1.start()
    t.fwd2_a()
    p0.diag1()
    q0.diag1()
    weight_grad(hid, bg, wd)
    dd_out = fetch(wd.at[pl.ds(0, hidden_n)], dd_hbm)
    p1.diag1()
    q1.diag1()
    t.fwd2_b()
    p0.sum1()
    q0.sum1()
    for chunk in range(4):
        dst = slice(128 * chunk, 128 * chunk + 128)
        ggt[:, dst] = gg[dst, :].astype(f32).T[:hidden_n].astype(bf)
        ugt[:, dst] = ug[dst, :].astype(f32).T[:hidden_n].astype(bf)
    p1.sum1()
    q1.sum1()
    p0.diag2()
    q0.diag2()
    p1.diag2()
    q1.diag2()
    p0.last()
    q0.last()
    p1.last()
    q1.last()
    t.done()
    weight_grad(ggt, bt, wg)
    dg_out = fetch(wg.at[pl.ds(0, hidden_n)], dg_hbm)
    weight_grad(ugt, bt, wu)
    du_out = fetch(wu.at[pl.ds(0, hidden_n)], du_hbm)

    pick_sent.wait_recv()
    arrived(p0.out + p1.out + q0.out + q1.out)
    took = jnp.where(sec == sections - 1, 0.0, pick_in[...].astype(f32)).T.astype(bf)
    step = 1024
    for c in range(0, width, step):
        rows = fin[:, :, c:c + step].reshape(2 * CAP, step)
        tok[:, c:c + step] = jnp.dot(took, rows, preferred_element_type=f32).astype(bf)
    arr_out = fetch(tok, arr_hbm)

    for c in remote:
        c.wait_send()
    for c in (dd_out, dg_out, du_out, arr_out):
        c.wait()


def exchange(ids, slots, gates, tok, og, sg, su, wg, wu, wd):
    width = tok.shape[-1]
    tokens_n = tok.shape[0]
    hidden_n = sg.shape[0]
    piece = width // 2 // PIECES
    f32, bf = jnp.float32, jnp.bfloat16
    rows_shape = (2, 2, 4, 2, CAP, width)
    padded = -(-hidden_n // 128) * 128
    any_spec = pl.BlockSpec(memory_space=pl.ANY)
    vm = pltpu.VMEM
    grad = jax.ShapeDtypeStruct((hidden_n, width), bf)
    return pl.pallas_call(
        kernel,
        name="exchange",
        out_shape=(jax.ShapeDtypeStruct((tokens_n, width), bf), grad, grad, grad),
        in_specs=[pl.BlockSpec(memory_space=pltpu.HBM)] * 10,
        out_specs=[any_spec] * 4,
        scratch_shapes=[
            vm(rows_shape, bf), vm(rows_shape, bf),
            vm((CAP, width), bf), vm((CAP, width), bf),
            vm(rows_shape, bf),
            vm((tokens_n, width), bf), vm((tokens_n, width), bf),
            vm((hidden_n, ROWS), bf), vm((hidden_n, ROWS), bf),
            vm((padded, width), bf), vm((padded, width), bf), vm((padded, width), bf),
            vm((ROWS, padded), f32), vm((ROWS, padded), f32), vm((ROWS, padded), f32),
            vm((ROWS, padded), bf), vm((ROWS, padded), bf),
            vm((hidden_n, ROWS), bf), vm((hidden_n, ROWS), bf), vm((hidden_n, ROWS), bf),
            vm((2, CAP, width), bf), vm((2, CAP, width), bf),
            vm((2 * CAP, tokens_n), bf), vm((2 * CAP, tokens_n), bf),
            vm(ids.shape, jnp.int32), vm(ids.shape, jnp.int32), vm(ids.shape, jnp.int32),
            vm((PIECES, 2, 2, 2, CAP, piece), bf), vm((PIECES, 2, 2, 2, 2, CAP, piece), bf),
            vm((PIECES, 2, 4, CAP, piece), bf), vm((PIECES, 2, 2, 4, CAP, piece), bf),
            vm((PIECES, 2, CAP, piece), bf), vm((PIECES, 2, 2, CAP, piece), bf),
            vm((PIECES, 2, CAP, piece), bf), vm((PIECES, 2, 2, CAP, piece), bf),
            pltpu.SemaphoreType.DMA((COPIES,)), pltpu.SemaphoreType.DMA((COPIES,)),
            pltpu.SemaphoreType.DMA((16,)),
        ],
        compiler_params=pltpu.CompilerParams(
            collective_id=0, has_side_effects=True, vmem_limit_bytes=VMEM_MIB << 20
        ),
        cost_estimate=pl.CostEstimate(
            flops=12 * ROWS * hidden_n * width, transcendentals=ROWS * hidden_n,
            bytes_accessed=24 << 20,
        ),
    )(ids, slots, gates, tok, og, sg, su, wg, wu, wd)


def store_kernel(*refs):
    ins, outs, sem = refs[:4], refs[4:8], refs[8]
    copies = []
    for src, dst in zip(ins, outs):
        rows = src.shape[0]
        for first in range(0, rows, rows // 2):
            part = pl.ds(first, rows // 2)
            copies.append(pltpu.make_async_copy(src.at[part], dst.at[part], sem.at[len(copies)]))
            copies[-1].start()
    for c in copies:
        c.wait()


def store(*arrays):
    size = sum(v.size for v in arrays)
    return pl.pallas_call(
        store_kernel,
        name="store",
        out_shape=tuple(jax.ShapeDtypeStruct(v.shape, v.dtype) for v in arrays),
        in_specs=[pl.BlockSpec(memory_space=pl.ANY)] * 4,
        out_specs=[pl.BlockSpec(memory_space=pltpu.HBM)] * 4,
        scratch_shapes=[pltpu.SemaphoreType.DMA((8,))],
        compiler_params=pltpu.CompilerParams(vmem_limit_bytes=1 << 20),
        cost_estimate=pl.CostEstimate(flops=0, transcendentals=0, bytes_accessed=4 * size),
    )(*arrays)


def shards(
    tokens, out_grad, expert_ids, slot_ids, gate_int, saved_gate, saved_up, w_gate, w_up, w_down
):
    arriving, grad_gate, grad_up, grad_down = exchange(
        *[pltpu.with_memory_space_constraint(v, pltpu.HBM) for v in (expert_ids[0].T, slot_ids[0].T, gate_int[0].T, tokens[0], out_grad[0],
        saved_gate[0].T, saved_up[0].T, w_gate[0].T, w_up[0].T, w_down[0])],
    )
    arriving, grad_gate, grad_up, grad_down = store(arriving, grad_gate, grad_up, grad_down)
    return (arriving[None], grad_gate.T[None], grad_up.T[None], grad_down[None])


def solution(mesh):
    row = P("section", "expert", None)
    col = P("section", None, "expert")
    return jax.shard_map(
        shards,
        mesh=mesh,
        in_specs=(row,) * 5 + (col,) * 4 + (row,),
        out_specs=(row, col, col, row),
        check_vma=False,
    )
```

time: 112 us -> 95.5 us (0.85)
  matrix products: 15.4 us -> 0 us
  starting transfers between devices: 10.4 us -> 0 us
  Pallas kernels: 83.4 us -> 93.5 us
    dot_general x4 -> x0, matrix products: 15.4 us -> none  [the longest x3 14.2 us: product(): jnp.dot(left, right, preferred_element_type=jnp.float32)]
    ppermute x3 -> x0, starting transfers between devices: 10.4 us -> none  [the longest x1 5.08 us: shards(): own = lax.ppermute(summed[0], axes, back)]
    pallas_call x1 -> x2, Pallas kernels: 83.4 us -> 93.5 us  [the longest x1 89.1 us: exchange(): pl.pallas_call(kernel, name='exchange', out_shape=(jax.ShapeDtypeStruct((...]
  transfers between devices with their start and end apart: 3 -> 0, of which waited for: 0 -> 0; matrix products, arithmetic and copies ran while one was open for 14% -> 0% of each run, Pallas kernels for 75% -> 0%
where the time goes in v2:
time: 95.5 us; the launch traced here: 94.1 us
  Pallas kernels  93.5 us (98%)
    pallas_call x1, Pallas kernels, exchange(): pl.pallas_call(kernel, name='exchange', out_shape=(jax.ShapeDtypeStruct((...  89.1 us
    pallas_call x1, Pallas kernels, store(): pl.pallas_call(store_kernel, name='store', out_shape=tuple((jax.ShapeDtyp...  4.34 us

profile of v2, /device:TPU:1, one launch (start us, length us, event | category | flops | bytes accessed | tf_op | source)
XLA Modules:
  0.0 94.1 jit_solution(10587827075110485660)
XLA Ops:
  0.6 89.1 %exchange.1 = (bf16[64,4096]{1,0:T(8,128)(2,1)S(1)}, bf16[448,4096]{1,0:T(8,128)(2,1)S(1)}, bf16[448,4096]{1,0:T(8,128)(2,1)S(1)}, bf16[448,4096]{1,0:T(8,128)(2,1)S(1)}) custom-call(s32[2,64]{1,0:T(2,128)} %bitcast.43, s32[2,64]{1,0:T(2,128)} %bitcast.44, s32[2,64]{1,0:T(2,128)} %bitcast.45, bf16[64,4096]{1,0:T(8,128)(2,1)} %bitcast.38, ...), custom_call_target="tpu_custom_call" | custom-call | flops 11274289152 | bytes 25165824 | tf_op jit(solution)/shard_map/exchange/pallas_call | solution.py:472
  89.8 4.3 %store.1 = (bf16[64,4096]{1,0:T(8,128)(2,1)}, bf16[448,4096]{1,0:T(8,128)(2,1)}, bf16[448,4096]{1,0:T(8,128)(2,1)}, bf16[448,4096]{1,0:T(8,128)(2,1)}) custom-call(bf16[64,4096]{1,0:T(8,128)(2,1)S(1)} %get-tuple-element.12.refs_0_, bf16[448,4096]{1,0:T(8,128)(2,1)S(1)} %get-tuple-element.13.refs_1_, bf16[448,4096]{1,0:T(8,128)(2,1)S(1)} %get-tuple-element.14.refs_2_, ...), custom_call_target="tpu_custom_call" | custom-call | bytes 23068672 | tf_op jit(solution)/shard_map/store/pallas_call | solution.py:523

commit v3 on v2

--- a/solution.py
+++ b/solution.py
@@ -65,9 +65,6 @@
     tok_in = fetch(tok_hbm, tok)
     sg_in = fetch(sg_hbm, sg)
     su_in = fetch(su_hbm, su)
-    wd_in = fetch(wd_hbm, wd.at[pl.ds(0, hidden_n)])
-    wg_in = fetch(wg_hbm, wg.at[pl.ds(0, hidden_n)])
-    wu_in = fetch(wu_hbm, wu.at[pl.ds(0, hidden_n)])
 
     barrier = pltpu.get_barrier_semaphore()
     for d in (y_dev, z_dev, xp_dev, xm_dev, c_dev, (after, e), (after, cross)):
@@ -185,17 +182,20 @@
     g = Gather(bg, cg)
     t = Gather(bt, ct)
     g.own()
+    wd_in = fetch(wd_hbm, wd.at[pl.ds(0, hidden_n)])
+    wg_in = fetch(wg_hbm, wg.at[pl.ds(0, hidden_n)])
+    wu_in = fetch(wu_hbm, wu.at[pl.ds(0, hidden_n)])
     tok_in.wait()
     place(pick, tok, bt, ct)
     t.own()
+    g.fwd1_a()
     g.crossed()
-    g.fwd1_a()
-    t.crossed()
     t.fwd1_a()
     g.fwd1_b()
     g.two_a()
+    t.crossed()
+    g.two_b()
     t.fwd1_b()
-    g.two_b()
 
     pick_sent = send(pick_out, pick_in, (before, e))
 
@@ -405,38 +405,38 @@
 
         lax.fori_loop(0, width // n_step, grad_step, 0)
 
-    p0, p1 = ScatterP(0), ScatterP(1)
-    q0, q1 = ScatterQ(0), ScatterQ(1)
+    ps = [ScatterP(k) for k in range(PIECES)]
+    qs = [ScatterQ(k) for k in range(PIECES)]
     wg_in.wait()
     wu_in.wait()
-    p0.start()
-    q0.start()
-    p1.start()
-    q1.start()
     t.fwd2_a()
-    p0.diag1()
-    q0.diag1()
+    ps[0].start()
+    qs[0].start()
+    ps[1].start()
+    qs[1].start()
+    ps[0].diag1()
+    qs[0].diag1()
+    ps[1].diag1()
+    qs[1].diag1()
+    t.fwd2_b()
     weight_grad(hid, bg, wd)
     dd_out = fetch(wd.at[pl.ds(0, hidden_n)], dd_hbm)
-    p1.diag1()
-    q1.diag1()
-    t.fwd2_b()
-    p0.sum1()
-    q0.sum1()
+    ps[0].sum1()
+    qs[0].sum1()
+    ps[1].sum1()
+    qs[1].sum1()
     for chunk in range(4):
         dst = slice(128 * chunk, 128 * chunk + 128)
         ggt[:, dst] = gg[dst, :].astype(f32).T[:hidden_n].astype(bf)
         ugt[:, dst] = ug[dst, :].astype(f32).T[:hidden_n].astype(bf)
-    p1.sum1()
-    q1.sum1()
-    p0.diag2()
-    q0.diag2()
-    p1.diag2()
-    q1.diag2()
-    p0.last()
-    q0.last()
-    p1.last()
-    q1.last()
+    ps[0].diag2()
+    qs[0].diag2()
+    ps[1].diag2()
+    qs[1].diag2()
+    ps[0].last()
+    qs[0].last()
+    ps[1].last()
+    qs[1].last()
     t.done()
     weight_grad(ggt, bt, wg)
     dg_out = fetch(wg.at[pl.ds(0, hidden_n)], dg_hbm)
@@ -444,7 +444,8 @@
     du_out = fetch(wu.at[pl.ds(0, hidden_n)], du_hbm)
 
     pick_sent.wait_recv()
-    arrived(p0.out + p1.out + q0.out + q1.out)
+    for scatter in ps + qs:
+        arrived(scatter.out)
     took = jnp.where(sec == sections - 1, 0.0, pick_in[...].astype(f32)).T.astype(bf)
     step = 1024
     for c in range(0, width, step):

time: 95.5 us -> 92.5 us (0.969); the launches traced: 94.1 us -> 92.1 us
  Pallas kernels: 93.5 us -> 91.5 us
    pallas_call x1, Pallas kernels: 89.1 us -> 87.1 us  [exchange(): pl.pallas_call(kernel, name='exchange', out_shape=(jax.ShapeDtypeStruct((...]
where the time goes in v3:
time: 92.5 us; the launch traced here: 92.1 us
  Pallas kernels  91.5 us (99%)
    pallas_call x1, Pallas kernels, exchange(): pl.pallas_call(kernel, name='exchange', out_shape=(jax.ShapeDtypeStruct((...  87.1 us
    pallas_call x1, Pallas kernels, store(): pl.pallas_call(store_kernel, name='store', out_shape=tuple((jax.ShapeDtyp...  4.34 us

profile of v3, /device:TPU:1, one launch (start us, length us, event | category | flops | bytes accessed | tf_op | source)
XLA Modules:
  0.0 92.1 jit_solution(274486081442750540)
XLA Ops:
  0.6 87.1 %exchange.1 = (bf16[64,4096]{1,0:T(8,128)(2,1)S(1)}, bf16[448,4096]{1,0:T(8,128)(2,1)S(1)}, bf16[448,4096]{1,0:T(8,128)(2,1)S(1)}, bf16[448,4096]{1,0:T(8,128)(2,1)S(1)}) custom-call(s32[2,64]{1,0:T(2,128)} %bitcast.43, s32[2,64]{1,0:T(2,128)} %bitcast.44, s32[2,64]{1,0:T(2,128)} %bitcast.45, bf16[64,4096]{1,0:T(8,128)(2,1)} %bitcast.38, ...), custom_call_target="tpu_custom_call" | custom-call | flops 11274289152 | bytes 25165824 | tf_op jit(solution)/shard_map/exchange/pallas_call | solution.py:473
  87.8 4.3 %store.1 = (bf16[64,4096]{1,0:T(8,128)(2,1)}, bf16[448,4096]{1,0:T(8,128)(2,1)}, bf16[448,4096]{1,0:T(8,128)(2,1)}, bf16[448,4096]{1,0:T(8,128)(2,1)}) custom-call(bf16[64,4096]{1,0:T(8,128)(2,1)S(1)} %get-tuple-element.12.refs_0_, bf16[448,4096]{1,0:T(8,128)(2,1)S(1)} %get-tuple-element.13.refs_1_, bf16[448,4096]{1,0:T(8,128)(2,1)S(1)} %get-tuple-element.14.refs_2_, ...), custom_call_target="tpu_custom_call" | custom-call | bytes 23068672 | tf_op jit(solution)/shard_map/store/pallas_call | solution.py:524

commit v4 on v3

--- a/solution.py
+++ b/solution.py
@@ -218,9 +218,9 @@
         buf[hidden_n:, :] = jnp.zeros((pad, width), bf)
 
     g.fwd2_a()
-    t.two_a()
     wd_in.wait()
     g.fwd2_b()
+    t.two_a()
     t.two_b()
     g.done()
 
@@ -395,7 +395,9 @@
                 ).astype(bf)
             self.out = to_before(c)
 
-    def weight_grad(left, rows, out):
+    stored = []
+
+    def weight_grad(left, rows, out, result, low, high):
 
         def grad_step(n, _):
             ns = pl.ds(pl.multiple_of(n * n_step, 128), n_step)
@@ -403,7 +405,9 @@
             out[pl.ds(0, hidden_n), ns] = jnp.dot(left[...], right, preferred_element_type=f32).astype(bf)
             return 0
 
-        lax.fori_loop(0, width // n_step, grad_step, 0)
+        lax.fori_loop(low * width // 4 // n_step, high * width // 4 // n_step, grad_step, 0)
+        done = pl.ds(low * width // 4, (high - low) * width // 4)
+        stored.append(fetch(out.at[pl.ds(0, hidden_n), done], result.at[:, done]))
 
     ps = [ScatterP(k) for k in range(PIECES)]
     qs = [ScatterQ(k) for k in range(PIECES)]
@@ -419,8 +423,7 @@
     ps[1].diag1()
     qs[1].diag1()
     t.fwd2_b()
-    weight_grad(hid, bg, wd)
-    dd_out = fetch(wd.at[pl.ds(0, hidden_n)], dd_hbm)
+    weight_grad(hid, bg, wd, dd_hbm, 0, 4)
     ps[0].sum1()
     qs[0].sum1()
     ps[1].sum1()
@@ -433,15 +436,15 @@
     qs[0].diag2()
     ps[1].diag2()
     qs[1].diag2()
+    t.done()
+    weight_grad(ggt, bt, wg, dg_hbm, 0, 2)
     ps[0].last()
     qs[0].last()
     ps[1].last()
     qs[1].last()
-    t.done()
-    weight_grad(ggt, bt, wg)
-    dg_out = fetch(wg.at[pl.ds(0, hidden_n)], dg_hbm)
-    weight_grad(ugt, bt, wu)
-    du_out = fetch(wu.at[pl.ds(0, hidden_n)], du_hbm)
+    weight_grad(ggt, bt, wg, dg_hbm, 2, 4)
+    weight_grad(ugt, bt, wu, du_hbm, 0, 2)
+    weight_grad(ugt, bt, wu, du_hbm, 2, 4)
 
     pick_sent.wait_recv()
     for scatter in ps + qs:
@@ -455,7 +458,7 @@
 
     for c in remote:
         c.wait_send()
-    for c in (dd_out, dg_out, du_out, arr_out):
+    for c in stored + [arr_out]:
         c.wait()
 
 
@@ -494,7 +497,7 @@
             vm((PIECES, 2, CAP, piece), bf), vm((PIECES, 2, 2, CAP, piece), bf),
             vm((PIECES, 2, CAP, piece), bf), vm((PIECES, 2, 2, CAP, piece), bf),
             pltpu.SemaphoreType.DMA((COPIES,)), pltpu.SemaphoreType.DMA((COPIES,)),
-            pltpu.SemaphoreType.DMA((16,)),
+            pltpu.SemaphoreType.DMA((24,)),
         ],
         compiler_params=pltpu.CompilerParams(
             collective_id=0, has_side_effects=True, vmem_limit_bytes=VMEM_MIB << 20

time: 92.5 us -> 90.8 us (0.982)
  Pallas kernels: 91.5 us -> 90 us
    pallas_call x1, Pallas kernels: 87.1 us -> 85.7 us  [exchange(): pl.pallas_call(kernel, name='exchange', out_shape=(jax.ShapeDtypeStruct((...]
where the time goes in v4:
time: 90.8 us; the launch traced here: 90.7 us
  Pallas kernels  90 us (99%)
    pallas_call x1, Pallas kernels, exchange(): pl.pallas_call(kernel, name='exchange', out_shape=(jax.ShapeDtypeStruct((...  85.7 us
    pallas_call x1, Pallas kernels, store(): pl.pallas_call(store_kernel, name='store', out_shape=tuple((jax.ShapeDtyp...  4.34 us

profile of v4, /device:TPU:1, one launch (start us, length us, event | category | flops | bytes accessed | tf_op | source)
XLA Modules:
  0.0 90.7 jit_solution(10993865088746294220)
XLA Ops:
  0.6 85.7 %exchange.1 = (bf16[64,4096]{1,0:T(8,128)(2,1)S(1)}, bf16[448,4096]{1,0:T(8,128)(2,1)S(1)}, bf16[448,4096]{1,0:T(8,128)(2,1)S(1)}, bf16[448,4096]{1,0:T(8,128)(2,1)S(1)}) custom-call(s32[2,64]{1,0:T(2,128)} %bitcast.43, s32[2,64]{1,0:T(2,128)} %bitcast.44, s32[2,64]{1,0:T(2,128)} %bitcast.45, bf16[64,4096]{1,0:T(8,128)(2,1)} %bitcast.38, ...), custom_call_target="tpu_custom_call" | custom-call | flops 11274289152 | bytes 25165824 | tf_op jit(solution)/shard_map/exchange/pallas_call | solution.py:476
  86.3 4.3 %store.1 = (bf16[64,4096]{1,0:T(8,128)(2,1)}, bf16[448,4096]{1,0:T(8,128)(2,1)}, bf16[448,4096]{1,0:T(8,128)(2,1)}, bf16[448,4096]{1,0:T(8,128)(2,1)}) custom-call(bf16[64,4096]{1,0:T(8,128)(2,1)S(1)} %get-tuple-element.12.refs_0_, bf16[448,4096]{1,0:T(8,128)(2,1)S(1)} %get-tuple-element.13.refs_1_, bf16[448,4096]{1,0:T(8,128)(2,1)S(1)} %get-tuple-element.14.refs_2_, ...), custom_call_target="tpu_custom_call" | custom-call | bytes 23068672 | tf_op jit(solution)/shard_map/store/pallas_call | solution.py:527
